TPU v7x, 32 devices: a whole 2x2x4 slice. The times are simulated.
32 devices in a mesh: dp: 16 (over z, y, x), vocab: 2 (over core).
Axes of the slice: x: 2, y: 2, z: 4, core: 2. Of those that a mesh axis runs over, the one named last changes fastest.
Arguments:
- tokens: int32 [144, 512], P('dp'), may hold values from 0 to 32127
- span_bounds: int32 [144, 16, 2], P('dp'), may hold values from 1 to 512, as said below
- owner: int32 [144, 80, 1], P('dp'), may hold values from 0 to 15; in each aligned block of 720 rows (0 to 719, 720 to 1439, ..., all dimensions but the last counted through in order) at most 48 rows name the same one
- decoder_states: bfloat16 [144, 80, 1024], P('dp', None, 'vocab'), may hold values from -1024 to 1024
- norm_gain: bfloat16 [1024], replicated, may hold values from 0.25 to 1.75
- embedding: bfloat16 [32128, 1024], P('vocab', 'dp'), may hold values from -64 to 64
Outputs:
- losses: float32 [12288], P('dp')
Inputs may be any that keep to these rules, and one draw needn't show every extreme that they name: `span_bounds`: within a sequence the 16 spans are disjoint and in increasing order, each with span_end - span_start from 1 to 5; every sequence has a span of exactly 5. Among the slots of one dp device no owner is named more than 48 times; in some of those blocks an owner is named exactly 48 times.
All inputs are finite; a program needn't handle non-finite values.
Results may differ from a plain program's by a relative error of at most 0.00047.
Values may be sent and summed in bfloat16 or wider, within the bound.
A program may use at most 128 MiB of HBM per device.

v0:
```python
import jax
import jax.numpy as jnp
from jax import lax
from jax.sharding import PartitionSpec as P

MAXSPAN = 5
OWN_ROWS = 768


epsilon = 1e-06


def normalize(rows, norm_gain):
    values = rows.astype(jnp.float32)
    mean_square = jnp.mean(values * values, axis=1, keepdims=True)
    scaled = (
        values
        * lax.rsqrt(mean_square + epsilon)
        * norm_gain.astype(jnp.float32)
        * values.shape[1] ** (-0.5)
    )
    return scaled.astype(jnp.bfloat16)


def on_device(tokens, span_bounds, owner, decoder_states, norm_gain, embedding):
    seq_count, slot_count, local_width = decoder_states.shape
    owner_total = lax.axis_size("dp")
    capacity = OWN_ROWS // owner_total
    slot_ids = jnp.arange(slot_count, dtype=jnp.int32)
    offsets = slot_ids % MAXSPAN
    starts = jnp.repeat(span_bounds[:, :, 0], MAXSPAN, axis=1)
    span_ends = jnp.repeat(span_bounds[:, :, 1], MAXSPAN, axis=1)
    is_live = (offsets[None, :] < span_ends - starts).reshape(-1)
    positions = jnp.minimum(starts + offsets[None, :], tokens.shape[1] - 1)
    labels = jnp.take_along_axis(tokens, positions, axis=1).reshape(-1)
    targets = owner.reshape(-1)
    slot_total = targets.shape[0]
    owner_hits = (targets[:, None] == jnp.arange(owner_total, dtype=jnp.int32)[None, :]).astype(
        jnp.bfloat16
    )
    device_slots = jnp.arange(slot_total, dtype=jnp.int32)
    earlier = (device_slots[:, None] > device_slots[None, :]).astype(jnp.bfloat16)
    running = jnp.dot(earlier, owner_hits, preferred_element_type=jnp.float32)
    slot_rank = jnp.sum(running * owner_hits.astype(jnp.float32), axis=1).astype(jnp.int32)
    target_row = targets * capacity + slot_rank
    placing = (target_row[None, :] == jnp.arange(OWN_ROWS, dtype=jnp.int32)[:, None]) & is_live[
        None, :
    ]
    sent_labels = jnp.sum(jnp.where(placing, labels[None, :] + 1, 0), axis=1) - 1
    onehot = placing.astype(jnp.bfloat16)
    states = decoder_states.reshape(slot_total, local_width)
    packed = jnp.dot(onehot, states, preferred_element_type=jnp.float32).astype(jnp.bfloat16)
    arrived, row_labels = (
        lax.all_to_all(
            packed.reshape(owner_total, capacity, local_width),
            "dp",
            split_axis=0,
            concat_axis=0,
            tiled=True,
        ),
        lax.all_to_all(
            sent_labels.reshape(owner_total, capacity),
            "dp",
            split_axis=0,
            concat_axis=0,
            tiled=True,
        ),
    )
    full_rows = lax.all_gather(arrived.reshape(OWN_ROWS, local_width), "vocab", axis=1, tiled=True)
    normed = normalize(full_rows, norm_gain)
    row_labels = row_labels.reshape(OWN_ROWS)
    vocab_rows = lax.all_gather(embedding, "dp", axis=1, tiled=True)
    logits = lax.dot_general(
        normed, vocab_rows, (((1,), (1,)), ((), ())), preferred_element_type=jnp.float32
    )
    shard_rows = vocab_rows.shape[0]
    local_label = row_labels - lax.axis_index("vocab") * shard_rows
    picked = jnp.sum(
        jnp.where(
            jnp.arange(shard_rows, dtype=jnp.int32)[None, :] == local_label[:, None], logits, 0.0
        ),
        axis=1,
    )
    local_top = jnp.max(logits, axis=1)
    row_top = lax.pmax(local_top, "vocab")
    exp_total, label_logit = lax.psum(
        (jnp.sum(jnp.exp(logits - row_top[:, None]), axis=1), picked), "vocab"
    )
    row_loss = row_top + jnp.log(exp_total) - label_logit
    return jnp.where(row_labels >= 0, row_loss, 0.0)


def solution(mesh):
    placed = (
        P("dp", None),
        P("dp", None, None),
        P("dp", None, None),
        P("dp", None, "vocab"),
        P(),
        P("vocab", "dp"),
    )
    return jax.shard_map(on_device, mesh=mesh, in_specs=placed, out_specs=P("dp"), check_vma=False)
```

profile of v0, /device:TPU:0, one launch (start us, length us, event | category | flops | bytes accessed | tf_op | source)
XLA Modules:
  0.0 467.9 jit_solution(1459183823252973298)
XLA Ops:
  6.5 0.0 copy-start
  6.5 0.0 all-gather.3.cloned.1.call-start
  6.6 0.1 lt.58
  6.6 0.8 reduce
  7.4 0.1 reshape.175
  7.5 0.3 fusion.17
  7.8 0.8 fusion.26
  8.6 0.1 broadcast_in_dim.43
  8.7 0.2 reshape.177
  8.9 0.1 broadcast_in_dim.42
  9.0 0.2 reshape.176
  9.2 0.0 copy-done
  9.2 1.1 fusion.13
  10.3 0.0 copy-start.2
  10.4 29.5 %all_to_all.11 = bf16[16,48,512]{2,1,0:T(8,128)(2,1)} all-to-all(bf16[16,48,512]{2,1,0:T(8,128)(2,1)S(1)} %bitcast.13), channel_id=1, replica_groups=mesh['dp'=16,'vocab'=2] {'dp'}, dimensions={0} | all-to-all | bytes 1572864 | tf_op jit(solution)/shard_map/all_to_all | solution.py:54
  39.9 0.0 all-gather.3.cloned.1.call-update
  39.9 0.0 all-gather.5.cloned.1.call-start
  40.0 0.7 all-gather.5.cloned.1.call-update
  40.7 0.1 reshape.178
  40.8 0.1 lt.61
  40.9 0.1 reshape.182
  40.9 0.0 copy-done.2
  40.9 0.0 copy-start.3
  41.0 9.9 %gather_fusion = s32[720]{0:T(1024)S(1)} fusion(s32[9,512]{1,0:T(8,128)S(1)} %copy-done.2, s32[720]{0:T(1024)S(1)} %reshape.182), kind=kCustom, calls=%fused_computation | custom fusion | bytes 11520 | tf_op jit(solution)/shard_map/jit(take_along_axis)/gather | solution.py:35
  50.9 0.7 select_reduce_fusion.1
  51.6 0.7 sub.39
  52.3 3.5 all-to-all-start
  55.8 0.0 copy-done.3
  55.8 7.2 %all-to-all-done = s32[16,1,48]{2,1,0:T(1,128)S(1)} async-done(((s32[16,1,48]{2,1,0:T(1,128)}), s32[16,1,48]{2,1,0:T(1,128)S(1)}, u32[]{:S(2)}, u32[]{:S(2)}) %all-to-all-start) | async-done | bytes 3104 | tf_op jit(solution)/shard_map/all_to_all | solution.py:61
  63.1 0.1 ge.26
  63.2 0.1 sub.44
  63.3 0.0 all-gather.3.cloned.1.call-done
  63.3 2.1 fusion
  65.4 331.6 %all-gather.5.cloned.1.call-done = bf16[16064,1024]{0,1:T(8,128)(2,1)} async-done(((bf16[16064,64]{0,1:T(8,128)(2,1)}), bf16[16064,1024]{0,1:T(8,128)(2,1)}) %all-gather.5.cloned.1.call-update) | async-done | bytes 32899088 | tf_op jit(solution)/shard_map/all_gather | solution.py:72
  396.9 36.8 %fusion.27 = (f32[768]{0:T(1024)S(1)}, f32[768,16064]{0,1:T(8,128)}) fusion(bf16[16064,1024]{0,1:T(8,128)(2,1)} %all-gather.5.cloned.1.call-done, bf16[768,1024]{1,0:T(8,128)(2,1)} %all-gather.3.cloned.1.call-done, f32[1024]{0:T(1024)S(1)} %convert_element_type.32, f32[768]{0:T(1024)S(1)} %add_rsqrt_fusion), kind=kOutput, calls=%fused_computation.47 | convolution fusion | flops 25282756608 | bytes 83830784 | tf_op jit(solution)/shard_map/dot_general | solution.py:73
  433.7 2.4 pmax.7
  436.2 0.0 copy-start.1
  436.2 21.8 %exponential_reduce_fusion = (f32[768]{0:T(1024)S(1)}, f32[768]{0:T(1024)S(1)}) fusion(f32[768,16064]{0,1:T(8,128)} %get-tuple-element.12, f32[768]{0:T(1024)S(1)} %pmax.7, s32[768]{0:T(1024)S(1)} %sub.44), kind=kLoop, calls=%fused_computation.3 | loop fusion | flops 61684224 | bytes 49360896 | tf_op jit(solution)/shard_map/reduce_sum | solution.py:87
  458.0 2.5 all-reduce
  460.5 0.6 subtract_select_fusion
  461.1 0.0 copy-done.1
  (13 shorter events, 0.1 us)
Async XLA Ops:
  6.5 2.7 copy-start
  6.5 56.7 %all-gather.3.cloned.1.call-start = ((), (), s32[]{:S(2)}) async-start(), calls=%async_computation.2 | async-start | bytes 2359296 | tf_op jit(solution)/shard_map/all_gather | solution.py:69
  10.3 30.6 %copy-start.2 = (s32[9,512]{1,0:T(8,128)S(1)}, s32[9,512]{1,0:T(8,128)}, u32[]{:S(2)}) copy-start(s32[9,512]{1,0:T(8,128)} %param.6) | copy-start | bytes 55300
  39.9 357.0 %all-gather.5.cloned.1.call-start = ((), (), s32[]{:S(2)}) async-start(), calls=%async_computation.3 | async-start | bytes 35094528 | tf_op jit(solution)/shard_map/all_gather | solution.py:72
  40.9 14.8 %copy-start.3 = (bf16[1024]{0:T(1024)(128)(2,1)S(1)}, bf16[1024]{0:T(1024)(128)(2,1)}, u32[]{:S(2)}) copy-start(bf16[1024]{0:T(1024)(128)(2,1)} %param.10) | copy-start | bytes 6148
  52.3 10.7 %all-to-all-start = ((s32[16,1,48]{2,1,0:T(1,128)}), s32[16,1,48]{2,1,0:T(1,128)S(1)}, u32[]{:S(2)}, u32[]{:S(2)}) async-start(s32[16,1,48]{2,1,0:T(1,128)} %sub.39), calls=%async_computation | async-start | bytes 16384 | tf_op jit(solution)/shard_map/all_to_all | solution.py:61
  436.2 24.9 %copy-start.1 = (bf16[9,80,512]{2,1,0:T(8,128)(2,1)S(1)}, bf16[9,80,512]{2,1,0:T(8,128)(2,1)}, u32[]{:S(2)}) copy-start(bf16[9,80,512]{2,1,0:T(8,128)(2,1)} %param.9) | copy-start | bytes 2211844
Sparse Core Ops, SparseCore 0:
  40.0 7.5 all-gather.2
  50.4 346.4 all-gather.4
where the time goes:
time: 469 us; the launch traced here: 468 us
  waiting for transfers between devices  340 us (72%)
  matrix products  38.3 us (8%)
  blocking collectives  34.5 us (7%)
  other arithmetic  26 us (6%)
  between operations  13.6 us (3%)
  local copies, waits for them, and re-layouts  12.6 us (3%)
    all_gather x1, waiting for transfers between devices, on_device(): vocab_rows = lax.all_gather(embedding, 'dp', axis=1, tiled=True)  332 us
    dot_general x1, matrix products, on_device(): lax.dot_general(normed, vocab_rows, (((1,), (1,)), ((), ())), preferred_e...  36.8 us
    all_to_all x1, blocking collectives, on_device(): lax.all_to_all(packed.reshape(owner_total, capacity, local_width), 'dp',...  29.5 us
    reduce_sum x1, other arithmetic, on_device(): jnp.sum(jnp.exp(logits - row_top[:, None]), axis=1)  21.8 us
    gather x2, local copies, waits for them, and re-layouts, on_device(): labels = jnp.take_along_axis(tokens, positions, axis=1).reshape(-1)  10 us
  transfers between devices with their start and end apart: 3, of which 2 were waited for; matrix products, arithmetic and copies ran while one was open for 3% of the time, Pallas kernels for 0%

commit v1 on v0

v1 whole, which is shorter than its diff:
```python
import functools

import jax
import jax.numpy as jnp
from jax import lax
from jax.experimental import pallas as pl
from jax.experimental.pallas import tpu as pltpu
from jax.sharding import PartitionSpec as P

MAXSPAN = 5
OWN_ROWS = 768
INNER = 4
LANES = 128
LOW = -1e30
MESH = pl.DeviceIdType.MESH


epsilon = 1e-06


def normalize(rows, norm_gain):
    values = rows.astype(jnp.float32)
    mean_square = jnp.mean(values * values, axis=1, keepdims=True)
    scaled = (
        values
        * lax.rsqrt(mean_square + epsilon)
        * norm_gain.astype(jnp.float32)
        * values.shape[1] ** (-0.5)
    )
    return scaled.astype(jnp.bfloat16)


def exchange_kernel(
    outer,
    inner,
    cores,
    chunk,
    rows_ref,
    labels_ref,
    table_ref,
    rows_out,
    labels_out,
    table_out,
    local_sem,
    table_send,
    table_recv,
    plane_send,
    plane_recv,
    rows_send,
    rows_recv,
    core_send,
    core_recv,
    label_send,
    label_recv,
):
    dp = lax.axis_index("dp")
    core = lax.axis_index("vocab")
    a = dp // inner
    b = lax.rem(dp, inner)

    def column(d):
        return (lax.rem(a + d, outer) * inner + b, core)

    def plane(e):
        return (a * inner + lax.rem(b + e, inner), core)

    def partner(f):
        return (dp, lax.rem(core + f, cores))

    barrier = pltpu.get_barrier_semaphore()
    greeted = (
        [column(d) for d in range(1, outer)]
        + [plane(e) for e in range(1, inner)]
        + [partner(f) for f in range(1, cores)]
    )
    for device in greeted:
        pl.semaphore_signal(barrier, inc=1, device_id=device, device_id_type=MESH)
    pl.semaphore_wait(barrier, len(greeted))

    def table_piece(index):
        return table_ref.at[:, pl.ds(pl.multiple_of(index * chunk, LANES), chunk)]

    def remote(src, dst, send, recv, device):
        return pltpu.make_async_remote_copy(
            src_ref=src,
            dst_ref=dst,
            send_sem=send,
            recv_sem=recv,
            device_id=device,
            device_id_type=MESH,
        )

    started = []
    arrive_table = {}
    arrive_rows = {}
    last = []
    for e in range(1, inner):
        copy = remote(
            table_piece(a), table_out.at[a, b], plane_send.at[0, e], plane_recv.at[0, e], plane(e)
        )
        copy.start()
        last.append(copy)
    for d in range(1, outer):
        copy = remote(
            table_piece(lax.rem(a + d, outer)),
            table_out.at[a, b],
            table_send.at[d],
            table_recv.at[d],
            column(d),
        )
        copy.start()
        arrive_table[d] = copy
    for f in range(1, cores):
        copy = remote(
            rows_ref, rows_out.at[a, core], core_send.at[0, f], core_recv.at[0, f], partner(f)
        )
        copy.start()
        last.append(copy)
    for d in range(1, outer):
        copy = remote(
            labels_ref, labels_out.at[a], label_send.at[d], label_recv.at[d], column(d)
        )
        copy.start()
        last.append(copy)
        copy = remote(
            rows_ref, rows_out.at[a, core], rows_send.at[d], rows_recv.at[d], column(d)
        )
        copy.start()
        arrive_rows[d] = copy
    local = [
        pltpu.make_async_copy(table_piece(a), table_out.at[a, b], local_sem.at[0]),
        pltpu.make_async_copy(rows_ref, rows_out.at[a, core], local_sem.at[1]),
        pltpu.make_async_copy(labels_ref, labels_out.at[a], local_sem.at[2]),
    ]
    for copy in local:
        copy.start()

    order = sorted(range(1, outer), key=lambda d: min(d, outer - d))
    for d in order:
        arrive_table[d].wait_recv()
        source = lax.rem(a + outer - d, outer)
        for e in range(1, inner):
            copy = remote(
                table_out.at[source, b],
                table_out.at[source, b],
                plane_send.at[d, e],
                plane_recv.at[d, e],
                plane(e),
            )
            copy.start()
            last.append(copy)
    for d in order:
        arrive_rows[d].wait_recv()
        source = lax.rem(a + outer - d, outer)
        for f in range(1, cores):
            copy = remote(
                rows_out.at[source, core],
                rows_out.at[source, core],
                core_send.at[d, f],
                core_recv.at[d, f],
                partner(f),
            )
            copy.start()
            last.append(copy)
    for copy in local:
        copy.wait()
    for d in order:
        arrive_table[d].wait_send()
        arrive_rows[d].wait_send()
    for copy in last:
        copy.wait()


def exchange(rows, labels, table, outer, inner, cores, chunk):
    any_space = pl.BlockSpec(memory_space=pl.ANY)
    dma = pltpu.SemaphoreType.DMA
    return pl.pallas_call(
        functools.partial(exchange_kernel, outer, inner, cores, chunk),
        out_shape=(
            jax.ShapeDtypeStruct((outer, cores) + rows.shape, rows.dtype),
            jax.ShapeDtypeStruct((outer,) + labels.shape, labels.dtype),
            jax.ShapeDtypeStruct((outer, inner, table.shape[0], chunk), table.dtype),
        ),
        in_specs=[any_space] * 3,
        out_specs=(any_space,) * 3,
        scratch_shapes=[
            dma((3,)),
            dma((outer,)),
            dma((outer,)),
            dma((outer, inner)),
            dma((outer, inner)),
            dma((outer,)),
            dma((outer,)),
            dma((outer, cores)),
            dma((outer, cores)),
            dma((outer,)),
            dma((outer,)),
        ],
        compiler_params=pltpu.CompilerParams(collective_id=0, has_side_effects=True),
    )(rows, labels, table)


def loss_kernel(block, shard_rows, limit_ref, rows_ref, labels_ref, table_ref, out_ref):
    rows = rows_ref[...]
    label = labels_ref[...]
    height = rows.shape[0]
    chunk = table_ref.shape[1]
    limit = limit_ref[0]
    start = limit_ref[1]
    top = jnp.full((height, 1), LOW, jnp.float32)
    total = jnp.zeros((height, 1), jnp.float32)
    picked = jnp.zeros((height, 1), jnp.float32)
    local_label = label - start
    for begin in range(0, chunk, block):
        logits = jnp.dot(
            rows, table_ref[:, begin : begin + block], preferred_element_type=jnp.float32
        )
        column = lax.broadcasted_iota(jnp.int32, (1, block), 1) + begin
        picked = picked + jnp.sum(
            jnp.where(column == local_label, logits, 0.0), axis=1, keepdims=True
        )
        logits = jnp.where(column < limit, logits, LOW)
        new_top = jnp.maximum(top, jnp.max(logits, axis=1, keepdims=True))
        total = total * jnp.exp(top - new_top) + jnp.sum(
            jnp.exp(logits - new_top), axis=1, keepdims=True
        )
        top = new_top
    total = jnp.where(label >= 0, total, 0.0)
    lane = lax.broadcasted_iota(jnp.int32, (height, LANES), 1)
    out_ref[...] = jnp.where(lane == 0, top, jnp.where(lane == 1, total, picked))


def partial_losses(rows, labels, table, limits, shard_rows):
    count, width = rows.shape
    chunk = table.shape[1]
    block = next(size for size in (1024, 512, 256, 128) if chunk % size == 0)
    height = 256
    return pl.pallas_call(
        functools.partial(loss_kernel, block, shard_rows),
        out_shape=jax.ShapeDtypeStruct((count, LANES), jnp.float32),
        grid=(count // height,),
        in_specs=[
            pl.BlockSpec(memory_space=pltpu.SMEM),
            pl.BlockSpec((height, width), lambda i: (i, 0)),
            pl.BlockSpec((height, 1), lambda i: (i, 0)),
            pl.BlockSpec((width, chunk), lambda i: (0, 0)),
        ],
        out_specs=pl.BlockSpec((height, LANES), lambda i: (i, 0)),
    )(limits, rows, labels, table)


def on_device(tokens, span_bounds, owner, decoder_states, norm_gain, embedding):
    seq_count, slot_count, local_width = decoder_states.shape
    owner_total = lax.axis_size("dp")
    cores = lax.axis_size("vocab")
    inner = INNER
    outer = owner_total // inner
    capacity = OWN_ROWS // owner_total
    shard_rows = embedding.shape[0]
    chunk = -(-shard_rows // (outer * LANES)) * LANES
    table = jnp.pad(embedding.T, ((0, 0), (0, outer * chunk - shard_rows)))

    slot_ids = jnp.arange(slot_count, dtype=jnp.int32)
    offsets = slot_ids % MAXSPAN
    starts = jnp.repeat(span_bounds[:, :, 0], MAXSPAN, axis=1)
    span_ends = jnp.repeat(span_bounds[:, :, 1], MAXSPAN, axis=1)
    is_live = (offsets[None, :] < span_ends - starts).reshape(-1)
    positions = jnp.minimum(starts + offsets[None, :], tokens.shape[1] - 1)
    here = positions[:, :, None] == jnp.arange(tokens.shape[1], dtype=jnp.int32)[None, None, :]
    labels = jnp.sum(jnp.where(here, tokens[:, None, :], 0), axis=2).reshape(-1)
    targets = owner.reshape(-1)
    slot_total = targets.shape[0]
    owner_hits = (targets[:, None] == jnp.arange(owner_total, dtype=jnp.int32)[None, :]).astype(
        jnp.bfloat16
    )
    device_slots = jnp.arange(slot_total, dtype=jnp.int32)
    earlier = (device_slots[:, None] > device_slots[None, :]).astype(jnp.bfloat16)
    running = jnp.dot(earlier, owner_hits, preferred_element_type=jnp.float32)
    slot_rank = jnp.sum(running * owner_hits.astype(jnp.float32), axis=1).astype(jnp.int32)
    target_row = targets * capacity + slot_rank
    placing = (target_row[None, :] == jnp.arange(OWN_ROWS, dtype=jnp.int32)[:, None]) & is_live[
        None, :
    ]
    sent_labels = jnp.sum(jnp.where(placing, labels[None, :] + 1, 0), axis=1) - 1
    onehot = placing.astype(jnp.bfloat16)
    states = decoder_states.reshape(slot_total, local_width)
    packed = jnp.dot(onehot, states, preferred_element_type=jnp.float32).astype(jnp.bfloat16)
    part = lax.all_to_all(packed, "vocab", split_axis=0, concat_axis=1, tiled=True)
    normed = normalize(part, norm_gain)

    label_tile = jnp.pad(sent_labels, (0, -OWN_ROWS % 1024)).reshape(-1, LANES)
    all_rows, all_labels, all_table = exchange(
        normed, label_tile, table, outer, inner, cores, chunk
    )
    rows = all_rows.reshape(outer * OWN_ROWS, -1)
    row_labels = all_labels.reshape(outer, -1)[:, :OWN_ROWS].reshape(-1, 1)
    full_table = all_table.reshape(rows.shape[1], chunk)
    first = lax.axis_index("dp") // inner * chunk
    limits = jnp.stack(
        [shard_rows - first, lax.axis_index("vocab") * shard_rows + first]
    ).astype(jnp.int32)
    out_of_range = row_labels - limits[1] >= limits[0]
    kept = jnp.where(out_of_range, shard_rows * cores + limits[1] + chunk, row_labels)
    partial = partial_losses(rows, kept, full_table, limits, shard_rows)

    values = partial[:, :3].reshape(outer, owner_total, capacity * 3)
    values = jnp.swapaxes(values, 0, 1).reshape(owner_total, 1, outer * capacity * 3)
    values = jnp.broadcast_to(values, (owner_total, cores, outer * capacity * 3))
    values = values.reshape(owner_total * cores, outer * capacity * 3)
    landed = lax.all_to_all(values, ("dp", "vocab"), split_axis=0, concat_axis=0, tiled=True)
    landed = landed.reshape(outer, inner, cores, outer, capacity, 3)
    tops, totals, picks = landed[..., 0], landed[..., 1], landed[..., 2]
    row_top = jnp.max(tops, axis=(0, 2))
    exp_total = jnp.sum(totals * jnp.exp(tops - row_top[None, :, None]), axis=(0, 2))
    label_logit = jnp.sum(picks, axis=(0, 2))
    row_loss = row_top + jnp.log(jnp.where(exp_total > 0.0, exp_total, 1.0)) - label_logit
    losses = jnp.where(exp_total > 0.0, row_loss, 0.0)
    return jnp.swapaxes(losses, 0, 1).reshape(-1)


def solution(mesh):
    placed = (
        P("dp", None),
        P("dp", None, None),
        P("dp", None, None),
        P("dp", None, "vocab"),
        P(),
        P("vocab", "dp"),
    )
    return jax.shard_map(on_device, mesh=mesh, in_specs=placed, out_specs=P("dp"), check_vma=False)
```

time: 469 us -> 219 us (0.47)
  waiting for transfers between devices: 340 us -> 0.01 us
  Pallas kernels: 0 us -> 149 us
  matrix products: 38.3 us -> 2.32 us
  between operations: 13.6 us -> 0.26 us
  other arithmetic: 26 us -> 13.2 us
    all_gather x2 -> x0, waiting for transfers between devices: 332 us -> none  [the longest x1 332 us: on_device(): vocab_rows = lax.all_gather(embedding, 'dp', axis=1, tiled=True)]
    pallas_call x0 -> x2, Pallas kernels: none -> 149 us  [the longest x1 107 us: exchange(): pl.pallas_call(functools.partial(exchange_kernel, outer, inner, cores, ch...]
    dot_general x1 -> x0, matrix products: 36.8 us -> none  [on_device(): lax.dot_general(normed, vocab_rows, (((1,), (1,)), ((), ())), preferred_e...]
    reduce_sum x1 -> x2, other arithmetic: 21.8 us -> 0.54 us  [the longest x1 0.49 us: on_device(): labels = jnp.sum(jnp.where(here, tokens[:, None, :], 0), axis=2).reshape(-1)]
    gather x2 -> x0, local copies, waits for them, and re-layouts: 10 us -> none  [on_device(): labels = jnp.take_along_axis(tokens, positions, axis=1).reshape(-1)]
    reshape x1 -> x4, local copies, waits for them, and re-layouts: 0.21 us -> 7.97 us  [the longest x1 4.75 us: on_device(): landed = landed.reshape(outer, inner, cores, outer, capacity, 3)]
    slice x0 -> x1, other arithmetic: none -> 7.45 us  [on_device(): tops, totals, picks = (landed[..., 0], landed[..., 1], landed[..., 2])]
    all_to_all x1, waiting for transfers between devices: 7.24 us -> 0.01 us  [on_device(): lax.all_to_all(packed, 'vocab', split_axis=0, concat_axis=1, tiled=True)]
  transfers between devices with their start and end apart: 3 -> 1, of which waited for: 2 -> 0; matrix products, arithmetic and copies ran while one was open for 3% -> 1% of each run, Pallas kernels for 0% -> 0%
where the time goes in v1:
time: 219 us
  Pallas kernels  149 us (68%)
  blocking collectives  36.7 us (17%)
  local copies, waits for them, and re-layouts  14.1 us (6%)
  other arithmetic  13.2 us (6%)
  starting transfers between devices  3.67 us (2%)
  matrix products  2.32 us (1%)
    pallas_call x1, Pallas kernels, exchange(): pl.pallas_call(functools.partial(exchange_kernel, outer, inner, cores, ch...  107 us
    pallas_call x1, Pallas kernels, partial_losses(): pl.pallas_call(functools.partial(loss_kernel, block, shard_rows), out_sha...  41.4 us
    all_to_all x1, blocking collectives, on_device(): lax.all_to_all(values, ('dp', 'vocab'), split_axis=0, concat_axis=0, tile...  36.7 us
    slice x1, other arithmetic, on_device(): tops, totals, picks = (landed[..., 0], landed[..., 1], landed[..., 2])  7.45 us
    reshape x1, local copies, waits for them, and re-layouts, on_device(): landed = landed.reshape(outer, inner, cores, outer, capacity, 3)  4.75 us
  transfers between devices with their start and end apart: 1, of which 0 were waited for; matrix products, arithmetic and copies ran while one was open for 1% of the time, Pallas kernels for 0%

profile of v1, /device:TPU:0, one launch (start us, length us, event | category | flops | bytes accessed | tf_op | source)
XLA Modules:
  0.0 218.7 jit_solution(14637373743140020256)
XLA Ops:
  0.0 0.0 copy-start
  0.0 0.1 lt.26
  0.1 0.8 reduce.4
  0.9 0.1 reshape.148
  0.9 0.3 fusion.10
  1.3 0.8 fusion.19
  2.1 0.1 broadcast_in_dim.59
  2.2 0.2 sub.51
  2.4 0.0 copy-done
  2.4 2.0 fusion.6
  4.4 0.0 copy-start.3
  4.4 0.0 copy-start.2
  4.4 3.7 %all-to-all-start = ((bf16[2,384,512]{2,1,0:T(8,128)(2,1)}), bf16[2,384,512]{2,1,0:T(8,128)(2,1)S(1)}, u32[]{:S(2)}, u32[]{:S(2)}) async-start(bf16[2,384,512]{2,1,0:T(8,128)(2,1)} %bitcast.5), calls=%async_computation | async-start | bytes 1572864 | tf_op jit(solution)/shard_map/all_to_all | solution.py:288
  8.1 0.0 copy-done.3
  8.1 0.1 broadcast_in_dim.60
  8.2 0.1 reshape.150
  8.3 0.0 copy-done.2
  8.3 0.5 select_reduce_fusion.1
  8.8 0.1 add.80
  8.9 0.7 select_reduce_fusion
  9.6 0.6 pad_bitcast_fusion.labels_ref
  10.2 0.0 all-to-all-done
  10.2 0.2 fusion.4
  10.4 0.2 convert_bitcast_fusion
  10.7 0.0 copy-start.1
  10.7 0.1 copy.40
  10.8 1.4 copy-done.1
  12.2 1.5 pad.9.table_ref
  13.7 1.1 multiply_convert_fusion.rows_ref
  14.8 107.1 %shard_map.64 = (bf16[4,2,384,1024]{3,2,1,0:T(8,128)(2,1)}, s32[4,8,128]{2,1,0:T(8,128)}, bf16[4,4,64,4096]{3,2,1,0:T(8,128)(2,1)}) custom-call(bf16[384,1024]{1,0:T(8,128)(2,1)} %multiply_convert_fusion.rows_ref, s32[8,128]{1,0:T(8,128)} %pad_bitcast_fusion.labels_ref, bf16[64,16384]{1,0:T(8,128)(2,1)} %pad.9.table_ref), custom_call_target="tpu_custom_call" | custom-call | tf_op jit(solution)/shard_map/pallas_call | solution.py:177
  122.0 0.7 copy.51
  122.7 0.5 copy.43
  123.3 0.6 pad_add_fusion.limit_ref
  123.8 1.4 bitcast_select_fusion.labels_ref
  125.2 41.4 %shard_map.65 = f32[3072,128]{1,0:T(8,128)} custom-call(s32[2]{0:T(128)} %pad_add_fusion.limit_ref, bf16[3072,1024]{1,0:T(8,128)(2,1)} %bitcast.48, s32[3072,1]{1,0:T(8,128)} %bitcast_select_fusion.labels_ref, bf16[1024,4096]{1,0:T(8,128)(2,1)} %bitcast.47), custom_call_target="tpu_custom_call" | custom-call | tf_op jit(solution)/shard_map/pallas_call | solution.py:238
  166.6 1.9 reshape.156
  168.6 0.1 broadcast_in_dim.66
  168.8 0.1 all_to_all.18
  168.9 36.7 %all_to_all.22 = f32[32,1,576]{2,1,0:T(1,128)S(1)} all-to-all(f32[32,1,576]{2,1,0:T(1,128)S(1)} %all_to_all.18), channel_id=1, replica_groups=mesh['dp'=16,'vocab'=2] {'dp','vocab'}, dimensions={0} | all-to-all | bytes 147456 | tf_op jit(solution)/shard_map/all_to_all | solution.py:310
  205.6 0.2 reduce.5
  205.8 4.8 %reshape.157 = f32[4,4,2,4,48,3]{5,4,3,2,1,0:T(8,128)} reshape(f32[32,576]{1,0:T(8,128)S(1)} %reduce.5) | data formatting | bytes 147456 | tf_op jit(solution)/shard_map/reshape | solution.py:311
  210.5 7.5 %slice_reduce_fusion.3 = (f32[4,4,2,4,48]{4,3,2,1,0:T(4,128)S(1)}, f32[4,4,48]{2,1,0:T(4,128)S(1)}, f32[4,4,48]{2,1,0:T(4,128)S(1)}, f32[4,4,2,4,48]{4,3,2,1,0:T(4,128)S(1)}) fusion(f32[4,4,2,4,48,3]{5,4,3,2,1,0:T(8,128)} %reshape.157), kind=kLoop, calls=%fused_computation.3 | loop fusion | flops 10752 | bytes 129024 | tf_op jit(solution)/shard_map/slice | solution.py:312
  218.1 0.7 reshape.158
  (18 shorter events, 0.2 us)
Async XLA Ops:
  0.0 2.4 %copy-start = (bf16[9,80,512]{2,1,0:T(8,128)(2,1)S(1)}, bf16[9,80,512]{2,1,0:T(8,128)(2,1)}, u32[]{:S(2)}) copy-start(bf16[9,80,512]{2,1,0:T(8,128)(2,1)} %param.9) | copy-start | bytes 2211844
  4.4 3.7 %copy-start.3 = (bf16[1024]{0:T(1024)(128)(2,1)S(1)}, bf16[1024]{0:T(1024)(128)(2,1)}, u32[]{:S(2)}) copy-start(bf16[1024]{0:T(1024)(128)(2,1)} %param.10) | copy-start | bytes 6148
  4.4 3.9 %copy-start.2 = (s32[9,512]{1,0:T(8,128)S(1)}, s32[9,512]{1,0:T(8,128)}, u32[]{:S(2)}) copy-start(s32[9,512]{1,0:T(8,128)} %param.6) | copy-start | bytes 55300
  4.4 5.8 %all-to-all-start = ((bf16[2,384,512]{2,1,0:T(8,128)(2,1)}), bf16[2,384,512]{2,1,0:T(8,128)(2,1)S(1)}, u32[]{:S(2)}, u32[]{:S(2)}) async-start(bf16[2,384,512]{2,1,0:T(8,128)(2,1)} %bitcast.5), calls=%async_computation | async-start | bytes 1572864 | tf_op jit(solution)/shard_map/all_to_all | solution.py:288
  10.7 1.6 copy-start.1

commit v2 on v0

v2 whole, which is shorter than its diff:
```python
import functools

import jax
import jax.numpy as jnp
from jax import lax
from jax.experimental import pallas as pl
from jax.experimental.pallas import tpu as pltpu
from jax.sharding import PartitionSpec as P

MAXSPAN = 5
OWN_ROWS = 768
INNER = 4
LANES = 128
LOW = -1e30
MESH = pl.DeviceIdType.MESH


epsilon = 1e-06


def normalize(rows, norm_gain):
    values = rows.astype(jnp.float32)
    mean_square = jnp.mean(values * values, axis=1, keepdims=True)
    scaled = (
        values
        * lax.rsqrt(mean_square + epsilon)
        * norm_gain.astype(jnp.float32)
        * values.shape[1] ** (-0.5)
    )
    return scaled.astype(jnp.bfloat16)


def exchange_loss_kernel(
    outer,
    inner,
    cores,
    chunk,
    block,
    limit,
    rows_ref,
    labels_ref,
    table_ref,
    out_ref,
    rows_vm,
    labels_vm,
    table_vm,
    stat_vm,
    local_sem,
    column_send,
    column_recv,
    ring_send,
    ring_recv,
    rows_send,
    rows_recv,
    core_send,
    core_recv,
    label_send,
    label_recv,
):
    dp = lax.axis_index("dp")
    core = lax.axis_index("vocab")
    a = dp // inner
    b = lax.rem(dp, inner)
    width = table_ref.shape[0]
    part = rows_ref.shape[0]
    per_source = part * cores
    stages = chunk // block

    def gray(p):
        return p + (p // 2) * (1 - 2 * lax.rem(p, 2))

    spot = gray(b)
    b_next = gray(lax.rem(spot + 1, inner))
    b_far = gray(lax.rem(spot + 2, inner))
    b_prev = gray(lax.rem(spot + inner - 1, inner))
    next_device = (a * inner + b_next, core)
    prev_device = (a * inner + b_prev, core)

    def column(d):
        return (lax.rem(a + d, outer) * inner + b, core)

    def partner(f):
        return (dp, lax.rem(core + f, cores))

    barrier = pltpu.get_barrier_semaphore()
    greeted = (
        [column(d) for d in range(1, outer)]
        + [next_device, prev_device]
        + [partner(f) for f in range(1, cores)]
    )
    for device in greeted:
        pl.semaphore_signal(barrier, inc=1, device_id=device, device_id_type=MESH)
    pl.semaphore_wait(barrier, len(greeted))

    def remote(src, dst, send, recv, device):
        return pltpu.make_async_remote_copy(
            src_ref=src,
            dst_ref=dst,
            send_sem=send,
            recv_sem=recv,
            device_id=device,
            device_id_type=MESH,
        )

    def origin(index, stage):
        return table_ref.at[
            :, pl.ds(pl.multiple_of(index * chunk + stage * block, LANES), block)
        ]

    def landed(row, col, stage):
        return table_vm.at[
            pl.ds(pl.multiple_of((row * inner + col) * width, width), width),
            pl.ds(stage * block, block),
        ]

    def behind(d):
        return lax.rem(a + outer - d, outer)

    def column_copy(d, s):
        return remote(
            origin(lax.rem(a + d, outer), s),
            landed(a, b, s),
            column_send.at[d, s],
            column_recv.at[d, s],
            column(d),
        )

    def ring_copy(kind, d, s):
        held_from = b if kind < 2 else (b_prev if kind == 2 else b_next)
        place = landed(behind(d), held_from, s)
        return remote(
            origin(a, s) if d == 0 and kind < 2 else place,
            place,
            ring_send.at[kind, d, s],
            ring_recv.at[kind, d, s],
            next_device if kind % 2 == 0 else prev_device,
        )

    def row_slot(source):
        return rows_vm.at[pl.ds(pl.multiple_of(source * per_source + core * part, 16), part), :]

    def row_copy(side, dist):
        source = a - dist if side == 0 else a + dist
        device = ((a + 1 if side == 0 else a - 1) * inner + b, core)
        return remote(
            rows_ref if dist == 0 else row_slot(source),
            row_slot(source),
            rows_send.at[side, dist],
            rows_recv.at[side, dist],
            device,
        )

    def core_copy(side, dist, f):
        source = a - dist if side == 0 else a + dist
        return remote(
            rows_ref if dist == 0 else row_slot(source),
            row_slot(source),
            core_send.at[side, dist, f],
            core_recv.at[side, dist, f],
            partner(f),
        )

    def label_copy(d):
        return remote(
            labels_ref, labels_vm.at[a], label_send.at[d], label_recv.at[d], column(d)
        )

    def has(side, dist):
        return a - dist >= 0 if side == 0 else a + dist < outer

    def goes_on(side):
        return a + 1 < outer if side == 0 else a >= 1

    def send_stage(s):
        for d in range(1, outer):
            column_copy(d, s).start()

    def ring_first(s):
        for d in range(1, outer):
            column_copy(d, s).wait_recv()
            for kind in (0, 1):
                ring_copy(kind, d, s).start()

    def ring_second(s):
        for d in range(outer):
            kind = d % 2
            ring_copy(kind, d, s).wait_recv()
            ring_copy(kind + 2, d, s).start()

    def ring_finish(s):
        for d in range(outer):
            ring_copy(1 - d % 2, d, s).wait_recv()
            ring_copy(d % 2 + 2, d, s).wait_recv()

    def row_arrive(dist):
        for side in (0, 1):

            @pl.when(has(side, dist))
            def _():
                row_copy(side, dist - 1).wait_recv()

                @pl.when(goes_on(side))
                def _():
                    row_copy(side, dist).start()

                for f in range(1, cores):
                    core_copy(side, dist, f).start()

    def row_finish(dist):
        for side in (0, 1):

            @pl.when(has(side, dist))
            def _():
                for f in range(1, cores):
                    core_copy(side, dist, f).wait_recv()

    local = [
        pltpu.make_async_copy(rows_ref, row_slot(a), local_sem.at[0]),
        pltpu.make_async_copy(labels_ref, labels_vm.at[a], local_sem.at[1]),
    ] + [
        pltpu.make_async_copy(origin(a, s), landed(a, b, s), local_sem.at[2 + s])
        for s in range(stages)
    ]
    early = min(2, stages)
    for s in range(early):
        send_stage(s)
    for d in range(1, outer):
        label_copy(d).start()
    for f in range(1, cores):
        core_copy(0, 0, f).start()
    for side in (0, 1):

        @pl.when(goes_on(side))
        def _():
            row_copy(side, 0).start()

    for s in range(early, stages):
        send_stage(s)
    for s in range(stages):
        for kind in (0, 1):
            if s < early:
                ring_copy(kind, 0, s).start()
    for copy in local:
        copy.start()

    eye = lax.broadcasted_iota(jnp.int32, (LANES, LANES), 0) == lax.broadcasted_iota(
        jnp.int32, (LANES, LANES), 1
    )
    height = 2 * LANES
    lane = lax.broadcasted_iota(jnp.int32, (height, LANES), 1)

    @pl.loop(0, stat_vm.shape[0] // height)
    def _(i):
        stat_vm[pl.ds(pl.multiple_of(i * height, height), height), :] = jnp.where(
            lane == 0, LOW, 0.0
        )

    first = a * chunk
    shift = core * limit + first

    def tile(source, begin, index):
        at = pl.ds(pl.multiple_of(source * per_source + index * height, height), height)
        wide = labels_vm[source, pl.ds(2 * index, 2), :]
        label = jnp.concatenate(
            [
                jnp.sum(jnp.where(eye, wide[h : h + 1, :], 0), axis=1, keepdims=True)
                for h in range(2)
            ],
            axis=0,
        )
        logits = jnp.dot(
            rows_vm[at, :],
            table_vm[:, pl.ds(begin, block)],
            preferred_element_type=jnp.float32,
        )
        col = lax.broadcasted_iota(jnp.int32, (1, block), 1) + begin
        stat = stat_vm[at, :]
        top, total, picked = stat[:, 0:1], stat[:, 1:2], stat[:, 2:3]
        inside = col + first < limit
        wanted = jnp.where(inside, col + shift, -2)
        picked = picked + jnp.sum(jnp.where(wanted == label, logits, 0.0), axis=1, keepdims=True)
        logits = jnp.where(inside, logits, LOW)
        new_top = jnp.maximum(top, jnp.max(logits, axis=1, keepdims=True))
        total = total * jnp.exp(top - new_top) + jnp.sum(
            jnp.exp(logits - new_top), axis=1, keepdims=True
        )
        total = jnp.where(label >= 0, total, 0.0)
        stat_vm[at, :] = jnp.where(lane == 0, new_top, jnp.where(lane == 1, total, picked))

    def compute(dist, low, high):
        @pl.loop(0, 1 if dist == 0 else 2)
        def _(side):
            source = a + (2 * side - 1) * dist

            @pl.when((source >= 0) & (source < outer))
            def _():
                @pl.loop(low, high)
                def _(s):
                    begin = pl.multiple_of(s * block, block)

                    @pl.loop(0, per_source // height)
                    def _(index):
                        tile(source, begin, index)

    for s in range(early):
        ring_first(s)
        if s == 0:
            ring_second(0)
    for copy in local:
        copy.wait()
    for f in range(1, cores):
        core_copy(0, 0, f).wait_recv()
    for d in range(1, outer):
        label_copy(d).wait_recv()
    ring_finish(0)
    done = [0] * outer
    reached = 1

    def catch_up(full):
        for dist in range(reached):
            if done[dist] < full:
                compute(dist, done[dist], full)
                done[dist] = full

    catch_up(1)
    row_arrive(1)
    reached = 2
    if stages > 1:
        ring_second(1)
    for s in range(early, stages):
        for kind in (0, 1):
            ring_copy(kind, 0, s).start()
    if stages > 2:
        ring_first(2)
    row_finish(1)
    if stages > 1:
        ring_finish(1)
    catch_up(min(2, stages))
    for s in range(2, stages):
        if s + 1 < stages:
            ring_first(s + 1)
        ring_second(s)
        if reached < outer and s > 2:
            row_arrive(reached)
            row_finish(reached)
            catch_up(s)
            reached += 1
            catch_up(s)
        ring_finish(s)
        catch_up(s + 1)
    while reached < outer:
        row_arrive(reached)
        row_finish(reached)
        reached += 1
        catch_up(stages)

    @pl.loop(0, outer * per_source // LANES)
    def _(i):
        stat = stat_vm[pl.ds(pl.multiple_of(i * LANES, LANES), LANES), :]
        for k in range(3):
            out_ref[k, pl.ds(i, 1), :] = jnp.sum(
                jnp.where(eye, stat[:, k : k + 1], 0.0), axis=0, keepdims=True
            )

    for s in range(stages):
        for d in range(1, outer):
            column_copy(d, s).wait_send()
        for d in range(outer):
            for kind in (0, 1, d % 2 + 2):
                ring_copy(kind, d, s).wait_send()
    for d in range(1, outer):
        label_copy(d).wait_send()
    for f in range(1, cores):
        core_copy(0, 0, f).wait_send()
    for side in (0, 1):

        @pl.when(goes_on(side))
        def _():
            row_copy(side, 0).wait_send()

        for dist in range(1, outer):

            @pl.when(has(side, dist))
            def _():
                @pl.when(goes_on(side))
                def _():
                    row_copy(side, dist).wait_send()

                for f in range(1, cores):
                    core_copy(side, dist, f).wait_send()


def partial_losses(rows, labels, table, outer, inner, cores, chunk, limit):
    block = next(size for size in (1024, 512, 256, 128) if chunk % size == 0)
    stages = chunk // block
    any_space = pl.BlockSpec(memory_space=pl.ANY)
    dma = pltpu.SemaphoreType.DMA
    count = outer * cores * rows.shape[0]
    width = rows.shape[1]
    return pl.pallas_call(
        functools.partial(exchange_loss_kernel, outer, inner, cores, chunk, block, limit),
        out_shape=jax.ShapeDtypeStruct((3, count // LANES, LANES), jnp.float32),
        in_specs=[any_space] * 3,
        out_specs=pl.BlockSpec(memory_space=pltpu.VMEM),
        scratch_shapes=[
            pltpu.VMEM((count, width), rows.dtype),
            pltpu.VMEM((outer,) + labels.shape, labels.dtype),
            pltpu.VMEM((width, chunk), table.dtype),
            pltpu.VMEM((count, LANES), jnp.float32),
            dma((2 + stages,)),
            dma((outer, stages)),
            dma((outer, stages)),
            dma((4, outer, stages)),
            dma((4, outer, stages)),
            dma((2, outer)),
            dma((2, outer)),
            dma((2, outer, cores)),
            dma((2, outer, cores)),
            dma((outer,)),
            dma((outer,)),
        ],
        compiler_params=pltpu.CompilerParams(collective_id=0, has_side_effects=True),
    )(rows, labels, table)


def on_device(tokens, span_bounds, owner, decoder_states, norm_gain, embedding):
    seq_count, slot_count, local_width = decoder_states.shape
    owner_total = lax.axis_size("dp")
    cores = lax.axis_size("vocab")
    inner = INNER
    outer = owner_total // inner
    capacity = OWN_ROWS // owner_total
    shard_rows = embedding.shape[0]
    chunk = -(-shard_rows // (outer * LANES)) * LANES
    table = jnp.pad(embedding.T, ((0, 0), (0, outer * chunk - shard_rows)))

    slot_ids = jnp.arange(slot_count, dtype=jnp.int32)
    offsets = slot_ids % MAXSPAN
    starts = jnp.repeat(span_bounds[:, :, 0], MAXSPAN, axis=1)
    span_ends = jnp.repeat(span_bounds[:, :, 1], MAXSPAN, axis=1)
    is_live = (offsets[None, :] < span_ends - starts).reshape(-1)
    positions = jnp.minimum(starts + offsets[None, :], tokens.shape[1] - 1)
    here = positions[:, :, None] == jnp.arange(tokens.shape[1], dtype=jnp.int32)[None, None, :]
    labels = jnp.sum(jnp.where(here, tokens[:, None, :], 0), axis=2).reshape(-1)
    targets = owner.reshape(-1)
    slot_total = targets.shape[0]
    owner_hits = (targets[:, None] == jnp.arange(owner_total, dtype=jnp.int32)[None, :]).astype(
        jnp.bfloat16
    )
    device_slots = jnp.arange(slot_total, dtype=jnp.int32)
    earlier = (device_slots[:, None] > device_slots[None, :]).astype(jnp.bfloat16)
    running = jnp.dot(earlier, owner_hits, preferred_element_type=jnp.float32)
    slot_rank = jnp.sum(running * owner_hits.astype(jnp.float32), axis=1).astype(jnp.int32)
    target_row = targets * capacity + slot_rank
    placing = (target_row[None, :] == jnp.arange(OWN_ROWS, dtype=jnp.int32)[:, None]) & is_live[
        None, :
    ]
    sent_labels = jnp.sum(jnp.where(placing, labels[None, :] + 1, 0), axis=1) - 1
    onehot = placing.astype(jnp.bfloat16)
    states = decoder_states.reshape(slot_total, local_width)
    packed = jnp.dot(onehot, states, preferred_element_type=jnp.float32).astype(jnp.bfloat16)
    part = lax.all_to_all(packed, "vocab", split_axis=0, concat_axis=1, tiled=True)
    normed = normalize(part, norm_gain)

    label_tile = jnp.pad(sent_labels, (0, -OWN_ROWS % 1024)).reshape(-1, LANES)
    partial = partial_losses(
        normed, label_tile, table, outer, inner, cores, chunk, shard_rows
    )

    size = 3 * outer * capacity
    values = partial.reshape(3, outer, owner_total, capacity)
    values = values.transpose(2, 0, 1, 3).reshape(owner_total, 1, size)
    values = jnp.broadcast_to(values, (owner_total, cores, size))
    values = values.reshape(owner_total * cores, size)
    landed = lax.all_to_all(values, ("dp", "vocab"), split_axis=0, concat_axis=0, tiled=True)
    landed = landed.reshape(outer, inner, cores, 3, outer, capacity)
    tops, totals, picks = landed[:, :, :, 0], landed[:, :, :, 1], landed[:, :, :, 2]
    row_top = jnp.max(tops, axis=(0, 2))
    exp_total = jnp.sum(totals * jnp.exp(tops - row_top[None, :, None]), axis=(0, 2))
    label_logit = jnp.sum(picks, axis=(0, 2))
    row_loss = row_top + jnp.log(jnp.where(exp_total > 0.0, exp_total, 1.0)) - label_logit
    losses = jnp.where(exp_total > 0.0, row_loss, 0.0)
    return jnp.swapaxes(losses, 0, 1).reshape(-1)


def solution(mesh):
    placed = (
        P("dp", None),
        P("dp", None, None),
        P("dp", None, None),
        P("dp", None, "vocab"),
        P(),
        P("vocab", "dp"),
    )
    return jax.shard_map(on_device, mesh=mesh, in_specs=placed, out_specs=P("dp"), check_vma=False)
```

time: 469 us -> 181 us (0.39)
  waiting for transfers between devices: 340 us -> 0.01 us
  Pallas kernels: 0 us -> 152 us
  matrix products: 38.3 us -> 2.32 us
  blocking collectives: 34.5 us -> 11.1 us
  other arithmetic: 26 us -> 3.85 us
  between operations: 13.6 us -> 0.23 us
  local copies, waits for them, and re-layouts: 12.6 us -> 7.15 us
    all_gather x2 -> x0, waiting for transfers between devices: 332 us -> none  [the longest x1 332 us: on_device(): vocab_rows = lax.all_gather(embedding, 'dp', axis=1, tiled=True)]
    pallas_call x0 -> x1, Pallas kernels: none -> 152 us  [partial_losses(): pl.pallas_call(functools.partial(exchange_loss_kernel, outer, inner, core...]
    dot_general x1 -> x0, matrix products: 36.8 us -> none  [on_device(): lax.dot_general(normed, vocab_rows, (((1,), (1,)), ((), ())), preferred_e...]
    reduce_sum x1 -> x2, other arithmetic: 21.8 us -> 0.54 us  [the longest x1 0.49 us: on_device(): labels = jnp.sum(jnp.where(here, tokens[:, None, :], 0), axis=2).reshape(-1)]
    all_to_all x1, blocking collectives: 29.5 us -> 11.1 us  [on_device(): lax.all_to_all(values, ('dp', 'vocab'), split_axis=0, concat_axis=0, tile...]
    gather x2 -> x0, local copies, waits for them, and re-layouts: 10 us -> none  [on_device(): labels = jnp.take_along_axis(tokens, positions, axis=1).reshape(-1)]
    all_to_all x1, waiting for transfers between devices: 7.24 us -> 0.01 us  [on_device(): lax.all_to_all(packed, 'vocab', split_axis=0, concat_axis=1, tiled=True)]
  transfers between devices with their start and end apart: 3 -> 1, of which waited for: 2 -> 0; matrix products, arithmetic and copies ran while one was open for 3% -> 1% of each run, Pallas kernels for 0% -> 0%
where the time goes in v2:
time: 181 us; the launch traced here: 180 us
  Pallas kernels  152 us (84%)
  blocking collectives  11.1 us (6%)
  local copies, waits for them, and re-layouts  7.15 us (4%)
  other arithmetic  3.85 us (2%)
  starting transfers between devices  3.67 us (2%)
  matrix products  2.32 us (1%)
    pallas_call x1, Pallas kernels, partial_losses(): pl.pallas_call(functools.partial(exchange_loss_kernel, outer, inner, core...  152 us
    all_to_all x1, blocking collectives, on_device(): lax.all_to_all(values, ('dp', 'vocab'), split_axis=0, concat_axis=0, tile...  11.1 us
    all_to_all x1, starting transfers between devices, on_device(): lax.all_to_all(packed, 'vocab', split_axis=0, concat_axis=1, tiled=True)  3.67 us
  transfers between devices with their start and end apart: 1, of which 0 were waited for; matrix products, arithmetic and copies ran while one was open for 1% of the time, Pallas kernels for 0%

profile of v2, /device:TPU:0, one launch (start us, length us, event | category | flops | bytes accessed | tf_op | source)
XLA Modules:
  0.0 180.4 jit_solution(13558465306646477655)
XLA Ops:
  0.0 0.0 copy-start
  0.0 0.1 lt.26
  0.1 0.8 reduce.4
  0.9 0.1 reshape.108
  0.9 0.3 fusion.9
  1.3 0.8 fusion.21
  2.1 0.1 broadcast_in_dim.55
  2.2 0.2 sub.28
  2.4 0.0 copy-done
  2.4 2.0 %fusion.5 = bf16[768,512]{1,0:T(8,128)(2,1)} fusion(bf16[720,512]{1,0:T(8,128)(2,1)S(1)} %bitcast.42, s32[720]{0:T(1024)S(1)} %convert_add_fusion, pred[720]{0:T(1024)(128)(4,1)S(1)} %lt.27), kind=kOutput, calls=%fused_computation.12 | convolution fusion | flops 567730176 | bytes 1527312 | tf_op jit(solution)/shard_map/dot_general | solution.py:461
  4.4 0.0 copy-start.3
  4.4 0.0 copy-start.2
  4.4 3.7 %all-to-all-start = ((bf16[2,384,512]{2,1,0:T(8,128)(2,1)}), bf16[2,384,512]{2,1,0:T(8,128)(2,1)S(1)}, u32[]{:S(2)}, u32[]{:S(2)}) async-start(bf16[2,384,512]{2,1,0:T(8,128)(2,1)} %bitcast.3), calls=%async_computation | async-start | bytes 1572864 | tf_op jit(solution)/shard_map/all_to_all | solution.py:462
  8.1 0.0 copy-done.3
  8.1 0.1 broadcast_in_dim.56
  8.2 0.1 reshape.110
  8.3 0.0 copy-done.2
  8.3 0.5 select_reduce_fusion.1
  8.8 0.1 add.70
  8.9 0.7 select_reduce_fusion
  9.6 0.6 pad_bitcast_fusion.labels_ref
  10.2 0.0 all-to-all-done
  10.2 0.2 fusion.4
  10.4 0.2 convert_bitcast_fusion
  10.6 0.0 copy-start.1
  10.6 0.1 copy.37
  10.8 1.4 copy-done.1
  12.2 1.5 pad.9.table_ref
  13.7 1.2 multiply_convert_fusion.rows_ref
  14.9 152.1 %shard_map.64 = f32[3,24,128]{2,1,0:T(8,128)} custom-call(bf16[384,1024]{1,0:T(8,128)(2,1)} %multiply_convert_fusion.rows_ref, s32[8,128]{1,0:T(8,128)} %pad_bitcast_fusion.labels_ref, bf16[64,16384]{1,0:T(8,128)(2,1)} %pad.9.table_ref), custom_call_target="tpu_custom_call" | custom-call | tf_op jit(solution)/shard_map/pallas_call | solution.py:400
  166.9 0.9 reshape.112
  167.8 0.1 broadcast_in_dim.61
  168.0 0.1 all_to_all.18
  168.1 11.1 %all_to_all.22 = f32[32,1,576]{2,1,0:T(1,128)S(1)} all-to-all(f32[32,1,576]{2,1,0:T(1,128)S(1)} %all_to_all.18), channel_id=1, replica_groups=mesh['dp'=16,'vocab'=2] {'dp','vocab'}, dimensions={0} | all-to-all | bytes 147456 | tf_op jit(solution)/shard_map/all_to_all | solution.py:475
  179.2 0.2 reduce.5
  179.4 0.2 reshape.113
  179.7 0.7 reshape.114
  (17 shorter events, 0.2 us)
Async XLA Ops:
  0.0 2.4 %copy-start = (bf16[9,80,512]{2,1,0:T(8,128)(2,1)S(1)}, bf16[9,80,512]{2,1,0:T(8,128)(2,1)}, u32[]{:S(2)}) copy-start(bf16[9,80,512]{2,1,0:T(8,128)(2,1)} %param.9) | copy-start | bytes 2211844
  4.4 3.7 %copy-start.3 = (bf16[1024]{0:T(1024)(128)(2,1)S(1)}, bf16[1024]{0:T(1024)(128)(2,1)}, u32[]{:S(2)}) copy-start(bf16[1024]{0:T(1024)(128)(2,1)} %param.10) | copy-start | bytes 6148
  4.4 3.9 %copy-start.2 = (s32[9,512]{1,0:T(8,128)S(1)}, s32[9,512]{1,0:T(8,128)}, u32[]{:S(2)}) copy-start(s32[9,512]{1,0:T(8,128)} %param.6) | copy-start | bytes 55300
  4.4 5.8 %all-to-all-start = ((bf16[2,384,512]{2,1,0:T(8,128)(2,1)}), bf16[2,384,512]{2,1,0:T(8,128)(2,1)S(1)}, u32[]{:S(2)}, u32[]{:S(2)}) async-start(bf16[2,384,512]{2,1,0:T(8,128)(2,1)} %bitcast.3), calls=%async_computation | async-start | bytes 1572864 | tf_op jit(solution)/shard_map/all_to_all | solution.py:462
  10.6 1.6 copy-start.1

commit v3 on v2

--- a/solution.py
+++ b/solution.py
@@ -247,13 +247,14 @@
         jnp.int32, (LANES, LANES), 1
     )
     height = 2 * LANES
-    lane = lax.broadcasted_iota(jnp.int32, (height, LANES), 1)
-
-    @pl.loop(0, stat_vm.shape[0] // height)
+    lane = lax.broadcasted_iota(jnp.int32, (1, LANES), 1)
+
+    @pl.loop(0, stat_vm.shape[1] // height)
     def _(i):
-        stat_vm[pl.ds(pl.multiple_of(i * height, height), height), :] = jnp.where(
-            lane == 0, LOW, 0.0
-        )
+        at = pl.ds(pl.multiple_of(i * height, height), height)
+        stat_vm[0, at, :] = jnp.full((height, LANES), LOW, jnp.float32)
+        stat_vm[1, at, :] = jnp.zeros((height, LANES), jnp.float32)
+        stat_vm[2, at, :] = jnp.zeros((height, LANES), jnp.float32)
 
     first = a * chunk
     shift = core * limit + first
@@ -273,19 +274,25 @@
             table_vm[:, pl.ds(begin, block)],
             preferred_element_type=jnp.float32,
         )
-        col = lax.broadcasted_iota(jnp.int32, (1, block), 1) + begin
-        stat = stat_vm[at, :]
-        top, total, picked = stat[:, 0:1], stat[:, 1:2], stat[:, 2:3]
-        inside = col + first < limit
-        wanted = jnp.where(inside, col + shift, -2)
-        picked = picked + jnp.sum(jnp.where(wanted == label, logits, 0.0), axis=1, keepdims=True)
-        logits = jnp.where(inside, logits, LOW)
-        new_top = jnp.maximum(top, jnp.max(logits, axis=1, keepdims=True))
-        total = total * jnp.exp(top - new_top) + jnp.sum(
-            jnp.exp(logits - new_top), axis=1, keepdims=True
-        )
-        total = jnp.where(label >= 0, total, 0.0)
-        stat_vm[at, :] = jnp.where(lane == 0, new_top, jnp.where(lane == 1, total, picked))
+        label = jnp.broadcast_to(label, (height, LANES))
+        top, total, picked = stat_vm[0, at, :], stat_vm[1, at, :], stat_vm[2, at, :]
+        new_top = top
+        pieces = []
+        for start in range(0, block, LANES):
+            piece = logits[:, start : start + LANES]
+            col = lane + (begin + start)
+            inside = col + first < limit
+            wanted = jnp.where(inside, col + shift, -2)
+            picked = picked + jnp.where(wanted == label, piece, 0.0)
+            piece = jnp.where(inside, piece, LOW)
+            new_top = jnp.maximum(new_top, piece)
+            pieces.append(piece)
+        total = total * jnp.exp(top - new_top)
+        for piece in pieces:
+            total = total + jnp.exp(piece - new_top)
+        stat_vm[0, at, :] = new_top
+        stat_vm[1, at, :] = total
+        stat_vm[2, at, :] = picked
 
     def compute(dist, low, high):
         @pl.loop(0, 1 if dist == 0 else 2)
@@ -298,7 +305,7 @@
                 def _(s):
                     begin = pl.multiple_of(s * block, block)
 
-                    @pl.loop(0, per_source // height)
+                    @pl.loop(0, per_source // height, unroll=True)
                     def _(index):
                         tile(source, begin, index)
 
@@ -354,13 +361,18 @@
         reached += 1
         catch_up(stages)
 
-    @pl.loop(0, outer * per_source // LANES)
+    groups = per_source // LANES
+
+    @pl.loop(0, outer * groups)
     def _(i):
-        stat = stat_vm[pl.ds(pl.multiple_of(i * LANES, LANES), LANES), :]
-        for k in range(3):
-            out_ref[k, pl.ds(i, 1), :] = jnp.sum(
-                jnp.where(eye, stat[:, k : k + 1], 0.0), axis=0, keepdims=True
-            )
+        at = pl.ds(pl.multiple_of(i * LANES, LANES), LANES)
+        top = jnp.max(stat_vm[0, at, :], axis=1, keepdims=True)
+        total = jnp.sum(stat_vm[1, at, :] * jnp.exp(stat_vm[0, at, :] - top), axis=1, keepdims=True)
+        picked = jnp.sum(stat_vm[2, at, :], axis=1, keepdims=True)
+        live = labels_vm[i // groups, pl.ds(lax.rem(i, groups), 1), :] >= 0
+        for k, value in enumerate((top, total, picked)):
+            row = jnp.sum(jnp.where(eye, value, 0.0), axis=0, keepdims=True)
+            out_ref[k, pl.ds(i, 1), :] = jnp.where(live, row, 0.0) if k == 1 else row
 
     for s in range(stages):
         for d in range(1, outer):
@@ -406,7 +418,7 @@
             pltpu.VMEM((count, width), rows.dtype),
             pltpu.VMEM((outer,) + labels.shape, labels.dtype),
             pltpu.VMEM((width, chunk), table.dtype),
-            pltpu.VMEM((count, LANES), jnp.float32),
+            pltpu.VMEM((3, count, LANES), jnp.float32),
             dma((2 + stages,)),
             dma((outer, stages)),
             dma((outer, stages)),

time: 181 us -> 165 us (0.912)
  Pallas kernels: 152 us -> 136 us
    pallas_call x1, Pallas kernels: 152 us -> 136 us  [partial_losses(): pl.pallas_call(functools.partial(exchange_loss_kernel, outer, inner, core...]
where the time goes in v3:
time: 165 us
  Pallas kernels  136 us (82%)
  blocking collectives  11.1 us (7%)
  local copies, waits for them, and re-layouts  7.15 us (4%)
  other arithmetic  3.85 us (2%)
  starting transfers between devices  3.67 us (2%)
  matrix products  2.32 us (1%)
    pallas_call x1, Pallas kernels, partial_losses(): pl.pallas_call(functools.partial(exchange_loss_kernel, outer, inner, core...  136 us
    all_to_all x1, blocking collectives, on_device(): lax.all_to_all(values, ('dp', 'vocab'), split_axis=0, concat_axis=0, tile...  11.1 us
    all_to_all x1, starting transfers between devices, on_device(): lax.all_to_all(packed, 'vocab', split_axis=0, concat_axis=1, tiled=True)  3.67 us
  transfers between devices with their start and end apart: 1, of which 0 were waited for; matrix products, arithmetic and copies ran while one was open for 1% of the time, Pallas kernels for 0%

profile of v3, /device:TPU:0, one launch (start us, length us, event | category | flops | bytes accessed | tf_op | source)
XLA Modules:
  0.0 164.7 jit_solution(23629338912182903)
XLA Ops:
  0.0 0.0 copy-start
  0.0 0.1 lt.26
  0.1 0.8 reduce.4
  0.9 0.1 reshape.108
  0.9 0.3 fusion.9
  1.3 0.8 fusion.21
  2.1 0.1 broadcast_in_dim.55
  2.2 0.2 sub.28
  2.4 0.0 copy-done
  2.4 2.0 %fusion.5 = bf16[768,512]{1,0:T(8,128)(2,1)} fusion(bf16[720,512]{1,0:T(8,128)(2,1)S(1)} %bitcast.42, s32[720]{0:T(1024)S(1)} %convert_add_fusion, pred[720]{0:T(1024)(128)(4,1)S(1)} %lt.27), kind=kOutput, calls=%fused_computation.12 | convolution fusion | flops 567730176 | bytes 1527312 | tf_op jit(solution)/shard_map/dot_general | solution.py:473
  4.4 0.0 copy-start.3
  4.4 0.0 copy-start.2
  4.4 3.7 %all-to-all-start = ((bf16[2,384,512]{2,1,0:T(8,128)(2,1)}), bf16[2,384,512]{2,1,0:T(8,128)(2,1)S(1)}, u32[]{:S(2)}, u32[]{:S(2)}) async-start(bf16[2,384,512]{2,1,0:T(8,128)(2,1)} %bitcast.3), calls=%async_computation | async-start | bytes 1572864 | tf_op jit(solution)/shard_map/all_to_all | solution.py:474
  8.1 0.0 copy-done.3
  8.1 0.1 broadcast_in_dim.56
  8.2 0.1 reshape.110
  8.3 0.0 copy-done.2
  8.3 0.5 select_reduce_fusion.1
  8.8 0.1 add.70
  8.9 0.7 select_reduce_fusion
  9.6 0.6 pad_bitcast_fusion.labels_ref
  10.2 0.0 all-to-all-done
  10.2 0.2 fusion.4
  10.4 0.2 convert_bitcast_fusion
  10.6 0.0 copy-start.1
  10.6 0.1 copy.37
  10.8 1.4 copy-done.1
  12.2 1.5 pad.9.table_ref
  13.7 1.2 multiply_convert_fusion.rows_ref
  14.9 136.4 %shard_map.64 = f32[3,24,128]{2,1,0:T(8,128)} custom-call(bf16[384,1024]{1,0:T(8,128)(2,1)} %multiply_convert_fusion.rows_ref, s32[8,128]{1,0:T(8,128)} %pad_bitcast_fusion.labels_ref, bf16[64,16384]{1,0:T(8,128)(2,1)} %pad.9.table_ref), custom_call_target="tpu_custom_call" | custom-call | tf_op jit(solution)/shard_map/pallas_call | solution.py:412
  151.2 0.9 reshape.112
  152.2 0.1 broadcast_in_dim.61
  152.3 0.1 all_to_all.18
  152.4 11.1 %all_to_all.22 = f32[32,1,576]{2,1,0:T(1,128)S(1)} all-to-all(f32[32,1,576]{2,1,0:T(1,128)S(1)} %all_to_all.18), channel_id=1, replica_groups=mesh['dp'=16,'vocab'=2] {'dp','vocab'}, dimensions={0} | all-to-all | bytes 147456 | tf_op jit(solution)/shard_map/all_to_all | solution.py:487
  163.6 0.2 reduce.5
  163.8 0.2 reshape.113
  164.0 0.7 reshape.114
  (17 shorter events, 0.2 us)
Async XLA Ops:
  0.0 2.4 %copy-start = (bf16[9,80,512]{2,1,0:T(8,128)(2,1)S(1)}, bf16[9,80,512]{2,1,0:T(8,128)(2,1)}, u32[]{:S(2)}) copy-start(bf16[9,80,512]{2,1,0:T(8,128)(2,1)} %param.9) | copy-start | bytes 2211844
  4.4 3.7 %copy-start.3 = (bf16[1024]{0:T(1024)(128)(2,1)S(1)}, bf16[1024]{0:T(1024)(128)(2,1)}, u32[]{:S(2)}) copy-start(bf16[1024]{0:T(1024)(128)(2,1)} %param.10) | copy-start | bytes 6148
  4.4 3.9 %copy-start.2 = (s32[9,512]{1,0:T(8,128)S(1)}, s32[9,512]{1,0:T(8,128)}, u32[]{:S(2)}) copy-start(s32[9,512]{1,0:T(8,128)} %param.6) | copy-start | bytes 55300
  4.4 5.8 %all-to-all-start = ((bf16[2,384,512]{2,1,0:T(8,128)(2,1)}), bf16[2,384,512]{2,1,0:T(8,128)(2,1)S(1)}, u32[]{:S(2)}, u32[]{:S(2)}) async-start(bf16[2,384,512]{2,1,0:T(8,128)(2,1)} %bitcast.3), calls=%async_computation | async-start | bytes 1572864 | tf_op jit(solution)/shard_map/all_to_all | solution.py:474
  10.6 1.6 copy-start.1
